TPU v7x, 32 devices: a whole 2x2x4 slice. The times are simulated.
32 devices in a mesh: blk: 4 (over z), sub: 8 (over y, x, core).
Axes of the slice: x: 2, y: 2, z: 4, core: 2. Of those that a mesh axis runs over, the one named last changes fastest.
Arguments:
- fields: float32 [32, 55, 2197], P(('blk', 'sub')), may hold values from -6 to 6
- flux_matrix: float32 [3, 55, 55], replicated, may hold values from -0.875 to 0.875
- inv_jacobian: float32 [32, 3], P(('blk', 'sub')), may hold values from 1 to 4
- neighbour: int32 [32, 6], P(('blk', 'sub')), may hold values from 0 to 31, as said below
- orientation: int32 [32, 6], P(('blk', 'sub')), may hold values from 0 to 7, as said below
- face_order: int32 [32, 6], P(('blk', 'sub')), may hold values from 9 to 13, as said below
Outputs:
- increment: float32 [32, 55, 2197], P(('blk', 'sub'))
Inputs may be any that keep to these rules, and one draw needn't show every extreme that they name: Element g belongs to the device with blk index (g) // 8 and sub index (g) % 8. The neighbour across face 0 (face 1) lies on the device one step lower (higher) along blk, cyclically, with the same sub index; across face 2 (face 3) on the device one step lower (higher) along sub, cyclically, with the same blk index; across faces 4 and 5 on the same device. If h = neighbour[g, f] then neighbour[h, f xor 1] = g, and the faces of one direction pair the elements of two devices one to one. `orientation`: the two sides of a face carry mutually inverse codes under orient. `face_order`: the two sides of a face carry the same order.
All inputs are finite; a program needn't handle non-finite values.
Results may differ from a plain program's by a relative error of at most 0.002.
Values may be sent and summed in bfloat16 or wider, within the bound.
A program may use at most 64 MiB of HBM per device.

v0:
```python
import jax
import jax.numpy as jnp
from jax import lax
from jax.sharding import PartitionSpec as P

PTS = 13


penalty = 1.0
time_step = 0.01
highest = lax.Precision.HIGHEST


def passed_along(block, axis, distance):
    devices = range(lax.axis_size(axis))
    route = [((i - distance) % len(devices), i) for i in devices]
    return lax.ppermute(block, axis, route)


def cheb_matrix(point_count):
    last_node = point_count - 1
    node_index = jnp.arange(point_count, dtype=jnp.int32)
    node_values = -jnp.cos(jnp.pi * node_index.astype(jnp.float32) / last_node)
    weights = jnp.where((node_index == 0) | (node_index == last_node), 2.0, 1.0) * jnp.where(
        node_index % 2 == 0, 1.0, -1.0
    )
    weights = weights.astype(jnp.float32)
    identity = jnp.eye(point_count, dtype=jnp.float32)
    node_gap = node_values[:, None] - node_values[None, :] + identity
    off_diag = weights[:, None] / weights[None, :] / node_gap * (1.0 - identity)
    return off_diag - jnp.diag(jnp.sum(off_diag, axis=1))


def dct_matrix(point_count):
    row_index = jnp.arange(point_count, dtype=jnp.float32)[:, None]
    col_index = jnp.arange(point_count, dtype=jnp.float32)[None, :]
    dct_basis = jnp.cos(jnp.pi * row_index * (col_index + 0.5) / point_count) * jnp.sqrt(
        2.0 / point_count
    )
    return dct_basis * jnp.where(row_index == 0, jnp.sqrt(0.5), 1.0).astype(jnp.float32)


def invert_code(face_code):
    turned = 4 + 2 * (face_code % 2) + face_code // 2 % 2
    return jnp.where(face_code >= 4, turned, face_code)


def orient_face(face_trace, face_code):
    shaped = face_code[:, None, None, None]
    flipped = jnp.where(shaped // 2 % 2 == 1, jnp.flip(face_trace, 2), face_trace)
    flipped = jnp.where(shaped % 2 == 1, jnp.flip(flipped, 3), flipped)
    return jnp.where(shaped >= 4, jnp.swapaxes(flipped, 2, 3), flipped)


def project(face_trace, mode_order, dct_basis):
    modes = jnp.einsum("ka,fvab,lb->fvkl", dct_basis, face_trace, dct_basis, precision=highest)
    mode_index = jnp.arange(dct_basis.shape[0], dtype=jnp.int32)
    keep = (mode_index[None, :] < mode_order[:, None]).astype(jnp.float32)
    mask_grid = keep[:, None, :, None] * keep[:, None, None, :]
    return jnp.einsum(
        "ka,fvkl,lb->fvab", dct_basis, modes * mask_grid, dct_basis, precision=highest
    )


def face_jump(own_trace, remote_trace, face_code, mode_order, dct_basis):
    turned = orient_face(remote_trace.astype(jnp.float32), face_code)
    return project(turned, mode_order, dct_basis) - project(
        own_trace.astype(jnp.float32), mode_order, dct_basis
    )


def apply_flux(matrix, jump_value):
    return jnp.einsum("wv,fvab->fwab", matrix, jump_value, precision=highest)


def face_traces(element_cube):
    last_index = element_cube.shape[-1] - 1
    return jnp.stack(
        [
            element_cube[:, :, 0],
            element_cube[:, :, last_index],
            element_cube[:, :, :, 0],
            element_cube[:, :, :, last_index],
            element_cube[:, :, :, :, 0],
            element_cube[:, :, :, :, last_index],
        ],
        axis=1,
    )


def volume_rate(element_cube, flux_matrix, inv_jacobian, derivative):
    along_x = jnp.einsum("ai,evijk->evajk", derivative, element_cube, precision=highest)
    along_y = jnp.einsum("aj,evijk->eviak", derivative, element_cube, precision=highest)
    along_z = jnp.einsum("ak,evijk->evija", derivative, element_cube, precision=highest)
    summed = jnp.zeros(element_cube.shape, jnp.float32)
    for axis_id, along in enumerate((along_x, along_y, along_z)):
        mixed = jnp.einsum("wv,evijk->ewijk", flux_matrix[axis_id], along, precision=highest)
        summed = summed + inv_jacobian[:, axis_id][:, None, None, None, None] * mixed
    return -summed


def add_faces(tendency, corrections, inv_jacobian, lift):
    last_index = tendency.shape[-1] - 1
    scaled = [
        corrections[face_id] * (lift * inv_jacobian[:, face_id // 2])[:, None, None, None]
        for face_id in range(6)
    ]
    tendency = tendency.at[:, :, 0].add(scaled[0])
    tendency = tendency.at[:, :, last_index].add(scaled[1])
    tendency = tendency.at[:, :, :, 0].add(scaled[2])
    tendency = tendency.at[:, :, :, last_index].add(scaled[3])
    tendency = tendency.at[:, :, :, :, 0].add(scaled[4])
    tendency = tendency.at[:, :, :, :, last_index].add(scaled[5])
    return tendency


def lower_face(traces, arrived, neighbour, orientation, face_order, matrix, dct_basis, low_face):
    elem_rows = traces.shape[0]
    slot_index = neighbour[:, low_face] % elem_rows
    jump_low = face_jump(
        traces[:, low_face],
        arrived[slot_index],
        orientation[:, low_face],
        face_order[:, low_face],
        dct_basis,
    )
    moved_low = apply_flux(matrix, jump_low)
    return (slot_index, jump_low, moved_low)


def returned_pair(traces, arrived, neighbour, orientation, face_order, matrix, dct_basis, low_face):
    slot_index, jump_low, moved_low = lower_face(
        traces, arrived, neighbour, orientation, face_order, matrix, dct_basis, low_face
    )
    corr_low = 0.5 * (penalty * jump_low + moved_low)
    sent_back = orient_face(
        0.5 * (moved_low - penalty * jump_low), invert_code(orientation[:, low_face])
    )
    placed = jnp.zeros_like(sent_back).at[slot_index].set(sent_back)
    return (corr_low, placed)


def upper_face(
    traces, arrived_back, neighbour, orientation, face_order, matrix, dct_basis, high_face
):
    elem_rows = traces.shape[0]
    slot_index = neighbour[:, high_face] % elem_rows
    jump_high = face_jump(
        traces[:, high_face],
        arrived_back[slot_index],
        orientation[:, high_face],
        face_order[:, high_face],
        dct_basis,
    )
    return 0.5 * (penalty * jump_high - apply_flux(matrix, jump_high))


def on_device(fields, flux_matrix, inv_jacobian, neighbour, orientation, face_order):
    elem_rows = fields.shape[0]
    width = fields.shape[1]
    element_cube = fields.reshape(elem_rows, width, PTS, PTS, PTS)
    derivative = cheb_matrix(PTS)
    dct_basis = dct_matrix(PTS)
    traces = face_traces(element_cube).astype(jnp.bfloat16)
    arrived_x = passed_along(traces[:, 1], "blk", 1)
    arrived_y = passed_along(traces[:, 3], "sub", 1)
    face_zero, placed_x = returned_pair(
        traces, arrived_x, neighbour, orientation, face_order, flux_matrix[0], dct_basis, 0
    )
    face_two, placed_y = returned_pair(
        traces, arrived_y, neighbour, orientation, face_order, flux_matrix[1], dct_basis, 2
    )
    face_one = passed_along(placed_x, "blk", -1)
    face_three = passed_along(placed_y, "sub", -1)
    slot_z, jump_z, moved_z = lower_face(
        traces, traces[:, 5], neighbour, orientation, face_order, flux_matrix[2], dct_basis, 4
    )
    face_four = 0.5 * (penalty * jump_z + moved_z)
    face_five = upper_face(
        traces, traces[:, 4], neighbour, orientation, face_order, flux_matrix[2], dct_basis, 5
    )
    tendency = volume_rate(element_cube, flux_matrix, inv_jacobian, derivative)
    tendency = add_faces(
        tendency,
        [face_zero, face_one, face_two, face_three, face_four, face_five],
        inv_jacobian,
        0.5 * (PTS - 1) ** 2,
    )
    return (time_step * tendency).reshape(elem_rows, width, PTS**3)


def solution(mesh):
    return jax.shard_map(
        on_device,
        mesh=mesh,
        in_specs=(
            P(("blk", "sub"), None, None),
            P(),
            P(("blk", "sub"), None),
            P(("blk", "sub"), None),
            P(("blk", "sub"), None),
            P(("blk", "sub"), None),
        ),
        out_specs=P(("blk", "sub"), None, None),
        check_vma=False,
    )
```

profile of v0, /device:TPU:0, one launch (start us, length us, event | category | flops | bytes accessed | tf_op | source)
XLA Modules:
  0.0 107.7 jit_solution(3298255804129403767)
XLA Ops:
  0.0 1.4 %convert.21 = bf16[1,55,2197]{2,0,1:T(2,128)(2,1)S(1)} convert(f32[1,55,2197]{2,0,1:T(1,128)} %param.22) | non-fusion elementwise | flops 120835 | bytes 725010 | tf_op jit(solution)/shard_map/convert.15
  1.4 0.8 copy.26
  2.4 0.6 slice_bitcast_fusion.4
  3.1 3.1 %collective-permute-start = (bf16[1,55,13,13]{1,3,2,0:T(8,128)(2,1)}, bf16[1,55,13,13]{1,3,2,0:T(8,128)(2,1)}, u32[]{:S(2)}, u32[]{:S(2)}) collective-permute-start(bf16[1,55,13,13]{1,3,2,0:T(8,128)(2,1)} %get-tuple-element.108), channel_id=1, source_target_pairs={{24,0},{0,8},{8,16},{16,24},{25,1},{1,9},{9,17},{17,25},{26,2},{2,... | collective-permute-start | bytes 55778 | tf_op jit(solution)/shard_map/ppermute | solution.py:17
  6.1 0.6 slice_bitcast_fusion.2
  6.8 0.8 copy.21
  7.9 2.4 %convolution_bitcast_fusion = f32[55,13,13,13]{0,3,2,1:T(8,128)} fusion(f32[55,13,13,13]{0,3,2,1:T(8,128)S(1)} %reshape.1012, f32[13]{0:T(128)S(1)} %fusion.270, f32[13]{0:T(128)S(1)} %get-tuple-element.133, f32[13]{0:T(128)S(1)} %get-tuple-element.132), kind=kOutput, calls=%fused_computation.1 | convolution fusion | flops 18851950 | bytes 966836 | tf_op jit(solution)/shard_map/ak,evijk->evija/dot_general | solution.py:94
  10.3 2.6 %convolution_bitcast_fusion.1 = f32[55,13,13,13]{0,2,3,1:T(8,128)} fusion(f32[55,13,13,13]{0,3,2,1:T(8,128)S(1)} %reshape.1012, f32[13]{0:T(128)S(1)} %fusion.270, f32[13]{0:T(128)S(1)} %get-tuple-element.133, f32[13]{0:T(128)S(1)} %get-tuple-element.132), kind=kOutput, calls=%fused_computation.3 | convolution fusion | flops 18851950 | bytes 966836 | tf_op jit(solution)/shard_map/aj,evijk->eviak/dot_general | solution.py:93
  13.0 1.5 %convolution_bitcast_fusion.2 = f32[55,13,13,13]{0,1,3,2:T(8,128)S(1)} fusion(f32[55,13,13,13]{0,3,2,1:T(8,128)S(1)} %reshape.1012, f32[13]{0:T(128)S(1)} %fusion.270, f32[13]{0:T(128)S(1)} %get-tuple-element.133, f32[13]{0:T(128)S(1)} %get-tuple-element.132), kind=kOutput, calls=%fused_computation.5 | convolution fusion | flops 18851950 | bytes 966836 | tf_op jit(solution)/shard_map/ai,evijk->evajk/dot_general | solution.py:92
  14.6 0.8 fusion.311
  15.4 0.7 fusion.313
  22.4 0.6 fusion.314
  23.0 0.4 fusion.68
  23.6 1.8 %fusion.14 = f32[55,13,13]{0,2,1:T(8,128)} fusion(f32[13,55,13]{2,1,0:T(8,128)S(1)} %copy.49, f32[13]{0:T(128)S(1)} %get-tuple-element.134, f32[13]{0:T(128)S(1)} %get-tuple-element.135, f32[13]{0:T(128)S(1)} %iota_multiply_fusion), kind=kOutput, calls=%fused_computation.27 | convolution fusion | flops 1450527 | bytes 74516 | tf_op jit(solution)/shard_map/ka,fvab,lb->fvkl/dot_general | solution.py:56
  25.5 0.6 fusion.312
  26.1 0.6 compare_convert_fusion.3
  26.8 0.4 fusion.66
  27.4 1.8 %fusion.12 = f32[55,13,13]{0,2,1:T(8,128)} fusion(f32[13,55,13]{2,1,0:T(8,128)S(1)} %copy.60, f32[13]{0:T(128)S(1)} %get-tuple-element.134, f32[13]{0:T(128)S(1)} %get-tuple-element.135, f32[13]{0:T(128)S(1)} %iota_multiply_fusion), kind=kOutput, calls=%fused_computation.25 | convolution fusion | flops 1450527 | bytes 74516 | tf_op jit(solution)/shard_map/ka,fvab,lb->fvkl/dot_general | solution.py:56
  29.2 0.6 compare_convert_fusion.2
  29.9 0.4 fusion.63
  30.5 1.2 %fusion.10 = f32[55,13,13]{0,2,1:T(8,128)S(1)} fusion(f32[13,55,13]{2,1,0:T(8,128)S(1)} %copy.71, f32[13]{0:T(128)S(1)} %get-tuple-element.134, f32[13]{0:T(128)S(1)} %get-tuple-element.135, f32[13]{0:T(128)S(1)} %iota_multiply_fusion), kind=kOutput, calls=%fused_computation.23 | convolution fusion | flops 1450527 | bytes 74516 | tf_op jit(solution)/shard_map/ka,fvab,lb->fvkl/dot_general | solution.py:56
  32.0 0.6 compare_convert_fusion.1
  33.0 0.4 fusion.29
  33.4 0.4 fusion.27
  34.8 1.0 fusion.44
  36.1 1.0 fusion.101
  37.0 0.4 fusion.60
  37.7 1.2 %fusion.8 = f32[55,13,13]{0,2,1:T(8,128)S(1)} fusion(f32[13,55,13]{2,1,0:T(8,128)S(1)} %copy.82, f32[13]{0:T(128)S(1)} %get-tuple-element.134, f32[13]{0:T(128)S(1)} %get-tuple-element.135, f32[13]{0:T(128)S(1)} %iota_multiply_fusion), kind=kOutput, calls=%fused_computation.21 | convolution fusion | flops 1450527 | bytes 74516 | tf_op jit(solution)/shard_map/ka,fvab,lb->fvkl/dot_general | solution.py:56
  39.1 0.6 compare_convert_fusion
  39.9 0.4 fusion.24
  40.3 0.4 fusion.22
  41.1 0.9 broadcast_multiply_fusion.1
  41.9 2.0 %copy.79 = f32[55,13,13]{0,1,2:T(8,128)} copy(f32[55,13,13]{2,1,0:T(8,128)} %get-tuple-element.110) | data formatting | bytes 74360 | tf_op jit(solution)/shard_map/mul | solution.py:61
  43.9 1.4 %fusion.96 = f32[55,13,13]{0,2,1:T(8,128)S(1)} fusion(f32[55,13,13]{0,1,2:T(8,128)} %copy.79, f32[13]{0:T(128)S(1)} %get-tuple-element.134, f32[13]{0:T(128)S(1)} %get-tuple-element.135, f32[13]{0:T(128)S(1)} %iota_multiply_fusion), kind=kOutput, calls=%fused_computation.155 | convolution fusion | flops 1450527 | bytes 74516 | tf_op jit(solution)/shard_map/ka,fvkl,lb->fvab/dot_general | solution.py:60
  45.3 1.0 fusion.41
  46.3 0.9 copy.84
  47.2 1.2 %fusion.91 = f32[55,13,13]{0,2,1:T(8,128)S(1)} fusion(f32[55,13,13]{0,1,2:T(8,128)} %copy.84, f32[13]{0:T(128)S(1)} %get-tuple-element.134, f32[13]{0:T(128)S(1)} %get-tuple-element.135, f32[13]{0:T(128)S(1)} %iota_multiply_fusion), kind=kOutput, calls=%fused_computation.150 | convolution fusion | flops 1450527 | bytes 74516 | tf_op jit(solution)/shard_map/ka,fvkl,lb->fvab/dot_general | solution.py:60
  48.4 1.3 %convolution_subtract_fusion.1 = f32[55,13,13]{0,2,1:T(8,128)S(1)} fusion(f32[55,13,13]{0,2,1:T(8,128)} %fusion.44, f32[55,13,13]{0,2,1:T(8,128)} %fusion.101, f32[13]{0:T(128)S(1)} %get-tuple-element.134, f32[13]{0:T(128)S(1)} %get-tuple-element.135, f32[13]{0:T(128)S(1)} %iota_multiply_fusion), kind=kOutput, calls=%fused_computation.15 | convolution fusion | flops 1459822 | bytes 111696 | tf_op jit(solution)/shard_map/ka,fvkl,lb->fvab/dot_general | solution.py:60
  49.8 0.9 fusion.76
  50.7 2.0 %convolution_multiply_fusion = f32[13,13,13,55]{3,2,1,0:T(8,128)S(1)} fusion(f32[55,13,13,13]{0,3,2,1:T(8,128)S(1)} %copy-done.1, f32[]{:T(128)} %bitcast.19, f32[3,55,55]{2,1,0:T(8,128)S(1)} %copy-done.3), kind=kOutput, calls=%fused_computation | convolution fusion | flops 79871944 | bytes 1896464 | tf_op jit(solution)/shard_map/wv,evijk->ewijk/dot_general | solution.py:97
  52.7 2.0 %convolution_multiply_fusion.1 = f32[13,13,13,55]{3,2,1,0:T(8,128)S(1)} fusion(f32[55,13,13,13]{0,2,3,1:T(8,128)S(1)} %copy-done, f32[]{:T(128)} %bitcast.10, f32[3,55,55]{2,1,0:T(8,128)S(1)} %copy-done.3), kind=kOutput, calls=%fused_computation.2 | convolution fusion | flops 79871944 | bytes 1896464 | tf_op jit(solution)/shard_map/wv,evijk->ewijk/dot_general | solution.py:97
  54.7 0.3 convolution_subtract_fusion
  55.1 3.0 %fusion.3 = f32[1,55,13,13,13]{1,4,3,2,0:T(8,128)S(1)} fusion(f32[13,13,13,55]{3,2,1,0:T(8,128)S(1)} %convolution_multiply_fusion, f32[13,13,13,55]{3,2,1,0:T(8,128)S(1)} %convolution_multiply_fusion.1, f32[55,13,13,13]{0,1,3,2:T(8,128)S(1)} %convolution_bitcast_fusion.2, f32[]{:T(128)} %bitcast, f32[3,55,55]{2,1,0:T(8,128)} %param.23), kind=kOutput, calls=%fused_computation.9 | convolution fusion | flops 80234448 | bytes 1962544 | tf_op jit(solution)/shard_map/wv,evijk->ewijk/dot_general | solution.py:97
  74.9 0.8 convert_element_type.133
  75.8 0.4 fusion.54
  76.2 0.4 fusion.37
  76.9 0.8 broadcast_multiply_fusion.7
  77.8 1.3 %copy.46 = f32[55,13,13]{0,1,2:T(8,128)S(1)} copy(f32[55,13,13]{2,1,0:T(8,128)} %get-tuple-element.116) | data formatting | bytes 74360 | tf_op jit(solution)/shard_map/mul | solution.py:61
  79.0 0.3 fusion.126
  80.0 0.3 fusion.121
  80.4 0.3 convolution_subtract_fusion.3
  80.7 1.0 fusion.21
  81.9 0.7 bitcast_select_fusion.1
  82.5 2.0 %collective-permute-start.1 = (f32[1,55,13,13]{1,3,2,0:T(8,128)}, f32[1,55,13,13]{1,3,2,0:T(8,128)}, u32[]{:S(2)}, u32[]{:S(2)}) collective-permute-start(f32[1,55,13,13]{1,3,2,0:T(8,128)} %bitcast_select_fusion.1), channel_id=1, source_target_pairs={{8,0},{16,8},{24,16},{0,24},{9,1},{17,9},{25,17},{1,25},{10,2},{18... | collective-permute-start | bytes 111548 | tf_op jit(solution)/shard_map/ppermute | solution.py:17
  84.6 0.8 convert_element_type.135
  85.5 0.4 fusion.49
  85.9 0.4 fusion.33
  88.7 1.0 fusion.20
  90.1 2.4 %collective-permute-start.3 = (f32[1,55,13,13]{1,3,2,0:T(8,128)S(1)}, f32[1,55,13,13]{1,3,2,0:T(8,128)S(1)}, u32[]{:S(2)}, u32[]{:S(2)}) collective-permute-start(f32[1,55,13,13]{1,3,2,0:T(8,128)S(1)} %copy_select_fusion), channel_id=1, source_target_pairs={{1,0},{2,1},{3,2},{4,3},{5,4},{6,5},{7,6},{0,7},{9,8},{10,9},{11,1... | collective-permute-start | bytes 111548 | tf_op jit(solution)/shard_map/ppermute | solution.py:17
  93.4 1.4 %collective-permute-done.3 = f32[1,55,13,13]{1,3,2,0:T(8,128)S(1)} collective-permute-done((f32[1,55,13,13]{1,3,2,0:T(8,128)S(1)}, f32[1,55,13,13]{1,3,2,0:T(8,128)S(1)}, u32[]{:S(2)}, u32[]{:S(2)}) %collective-permute-start.3) | collective-permute-done | bytes 37212 | tf_op jit(solution)/shard_map/ppermute | solution.py:17
  95.0 4.5 %scatter-add.26 = f32[1,55,13,13,13]{1,4,3,2,0:T(8,128)S(1)} dynamic-update-slice(f32[1,55,13,13,13]{1,4,3,2,0:T(8,128)S(1)} %fusion.16, f32[1,55,13,13,1]{1,4,3,2,0:T(1,128)S(1)} %fusion.57, s32[]{:T(128)} %constant.491.clone.1, s32[]{:T(128)} %constant.491.clone.1, s32[]{:T(128)} %constant.491.clone.1, s32[]{:T(128)} %constant.491.clone.1, s32[]{:T(128)} %constant.491.clone.1) | dynamic-update-slice | bytes 74364 | tf_op jit(solution)/shard_map/scatter-add | solution.py:112
  99.7 4.3 %scatter-add.29 = f32[1,55,13,13,13]{1,4,3,2,0:T(8,128)S(1)} dynamic-update-slice(f32[1,55,13,13,13]{1,4,3,2,0:T(8,128)S(1)} %scatter-add.26, f32[1,55,13,13,1]{1,4,3,2,0:T(1,128)S(1)} %slice_add_fusion.3, s32[]{:T(128)} %constant.491.clone.1, s32[]{:T(128)} %constant.491.clone.1, s32[]{:T(128)} %constant.491.clone.1, s32[]{:T(128)} %constant.491.clone.1, s32[]{:T(128)} %constant.492.clone.1) | dynamic-update-slice | bytes 74364 | tf_op jit(solution)/shard_map/scatter-add | solution.py:113
  104.1 1.1 %reshape.1030 = f32[1,55,2197]{1,0,2:T(1,128)S(1)} reshape(f32[1,55,13,13,13]{1,4,3,2,0:T(8,128)S(1)} %broadcast_multiply_fusion) | data formatting | bytes 966680 | tf_op jit(solution)/shard_map/reshape | solution.py:189
  105.2 2.4 %copy.37 = f32[1,55,2197]{2,0,1:T(1,128)} copy(f32[1,55,2197]{1,0,2:T(1,128)S(1)} %reshape.1030) | data formatting | bytes 966680 | tf_op jit(solution)/shard_map/reshape | solution.py:189
  (95 shorter events, 9.7 us)
Async XLA Ops:
  1.4 5.4 %copy-start.2 = (f32[1,55,2197]{2,0,1:T(1,128)S(1)}, f32[1,55,2197]{2,0,1:T(1,128)}, u32[]{:S(2)}) copy-start(f32[1,55,2197]{2,0,1:T(1,128)} %param.22) | copy-start | bytes 1450024
  3.1 71.8 %collective-permute-start = (bf16[1,55,13,13]{1,3,2,0:T(8,128)(2,1)}, bf16[1,55,13,13]{1,3,2,0:T(8,128)(2,1)}, u32[]{:S(2)}, u32[]{:S(2)}) collective-permute-start(bf16[1,55,13,13]{1,3,2,0:T(8,128)(2,1)} %get-tuple-element.108), channel_id=1, source_target_pairs={{24,0},{0,8},{8,16},{16,24},{25,1},{1,9},{9,17},{17,25},{26,2},{2,... | collective-permute-start | bytes 55778 | tf_op jit(solution)/shard_map/ppermute | solution.py:17
  6.7 77.8 %collective-permute-start.2 = (bf16[1,55,13,13]{1,3,2,0:T(8,128)(2,1)}, bf16[1,55,13,13]{1,3,2,0:T(8,128)(2,1)}, u32[]{:S(2)}, u32[]{:S(2)}) collective-permute-start(bf16[1,55,13,13]{1,3,2,0:T(8,128)(2,1)} %get-tuple-element.106), channel_id=1, source_target_pairs={{7,0},{0,1},{1,2},{2,3},{3,4},{4,5},{5,6},{6,7},{15,8},{8,9},{9,10... | collective-permute-start | bytes 55778 | tf_op jit(solution)/shard_map/ppermute | solution.py:17
  13.0 2.4 %copy-start.11 = (s32[1,6]{1,0:T(1,128)S(1)}, s32[1,6]{1,0:T(1,128)}, u32[]{:S(2)}) copy-start(s32[1,6]{1,0:T(1,128)} %param.25) | copy-start | bytes 76
  13.0 9.4 %copy-start.13 = (f32[1,3]{1,0:T(1,128)S(1)}, f32[1,3]{1,0:T(1,128)}, u32[]{:S(2)}) copy-start(f32[1,3]{1,0:T(1,128)} %param.24) | copy-start | bytes 40
  13.0 10.0 %copy-start.10 = (bf16[55,13,13]{0,2,1:T(8,128)(2,1)S(1)}, bf16[55,13,13]{0,2,1:T(8,128)(2,1)}, u32[]{:S(2)}) copy-start(bf16[55,13,13]{0,2,1:T(8,128)(2,1)} %get-tuple-element.107) | copy-start | bytes 55774
  14.6 10.9 %copy-start.12 = (s32[1,6]{1,0:T(1,128)S(1)}, s32[1,6]{1,0:T(1,128)}, u32[]{:S(2)}) copy-start(s32[1,6]{1,0:T(1,128)} %param.26) | copy-start | bytes 76
  34.1 2.9 %copy-start.9 = (bf16[1,55,13,13,1]{1,4,3,2,0:T(2,128)(2,1)S(1)}, bf16[1,55,13,13,1]{1,4,3,2,0:T(2,128)(2,1)}, u32[]{:S(2)}) copy-start(bf16[1,55,13,13,1]{1,4,3,2,0:T(2,128)(2,1)} %get-tuple-element.101) | copy-start | bytes 55774
  41.9 7.8 %copy-start.3 = (f32[3,55,55]{2,1,0:T(8,128)S(1)}, f32[3,55,55]{2,1,0:T(8,128)}, u32[]{:S(2)}) copy-start(f32[3,55,55]{2,1,0:T(8,128)} %param.23) | copy-start | bytes 108904
  41.9 8.7 %copy-start.1 = (f32[55,13,13,13]{0,3,2,1:T(8,128)S(1)}, f32[55,13,13,13]{0,3,2,1:T(8,128)}, u32[]{:S(2)}) copy-start(f32[55,13,13,13]{0,3,2,1:T(8,128)} %convolution_bitcast_fusion) | copy-start | bytes 1450024
  50.7 2.0 %copy-start = (f32[55,13,13,13]{0,2,3,1:T(8,128)S(1)}, f32[55,13,13,13]{0,2,3,1:T(8,128)}, u32[]{:S(2)}) copy-start(f32[55,13,13,13]{0,2,3,1:T(8,128)} %convolution_bitcast_fusion.1) | copy-start | bytes 1450024
  52.7 2.1 %copy-start.5 = (f32[55,13,13]{0,2,1:T(8,128)S(1)}, f32[55,13,13]{0,2,1:T(8,128)}, u32[]{:S(2)}) copy-start(f32[55,13,13]{0,2,1:T(8,128)} %fusion.41) | copy-start | bytes 111544
  55.1 19.0 %copy-start.8 = (f32[55,13,13]{0,2,1:T(8,128)S(1)}, f32[55,13,13]{0,2,1:T(8,128)}, u32[]{:S(2)}) copy-start(f32[55,13,13]{0,2,1:T(8,128)} %fusion.14) | copy-start | bytes 111544
  55.1 19.4 %copy-start.7 = (f32[55,13,13]{0,2,1:T(8,128)S(1)}, f32[55,13,13]{0,2,1:T(8,128)}, u32[]{:S(2)}) copy-start(f32[55,13,13]{0,2,1:T(8,128)} %fusion.12) | copy-start | bytes 111544
  82.5 6.1 %collective-permute-start.1 = (f32[1,55,13,13]{1,3,2,0:T(8,128)}, f32[1,55,13,13]{1,3,2,0:T(8,128)}, u32[]{:S(2)}, u32[]{:S(2)}) collective-permute-start(f32[1,55,13,13]{1,3,2,0:T(8,128)} %bitcast_select_fusion.1), channel_id=1, source_target_pairs={{8,0},{16,8},{24,16},{0,24},{9,1},{17,9},{25,17},{1,25},{10,2},{18... | collective-permute-start | bytes 111548 | tf_op jit(solution)/shard_map/ppermute | solution.py:17
  86.7 2.9 %copy-start.4 = (f32[3,55,55]{2,1,0:T(8,128)S(1)}, f32[3,55,55]{2,1,0:T(8,128)}, u32[]{:S(2)}) copy-start(f32[3,55,55]{2,1,0:T(8,128)} %param.23) | copy-start | bytes 108904
  88.7 6.2 %copy-start.6 = (f32[13,13,55]{2,1,0:T(8,128)S(1)}, f32[13,13,55]{2,1,0:T(8,128)}, u32[]{:S(2)}) copy-start(f32[13,13,55]{2,1,0:T(8,128)} %fusion.76) | copy-start | bytes 111544
  90.1 4.7 %collective-permute-start.3 = (f32[1,55,13,13]{1,3,2,0:T(8,128)S(1)}, f32[1,55,13,13]{1,3,2,0:T(8,128)S(1)}, u32[]{:S(2)}, u32[]{:S(2)}) collective-permute-start(f32[1,55,13,13]{1,3,2,0:T(8,128)S(1)} %copy_select_fusion), channel_id=1, source_target_pairs={{1,0},{2,1},{3,2},{4,3},{5,4},{6,5},{7,6},{0,7},{9,8},{10,9},{11,1... | collective-permute-start | bytes 111548 | tf_op jit(solution)/shard_map/ppermute | solution.py:17
where the time goes:
time: 109 us; the launch traced here: 108 us
  matrix products  37.1 us (34%)
  local copies, waits for them, and re-layouts  26.6 us (24%)
  between operations  23.7 us (22%)
  other arithmetic  11.4 us (10%)
  starting transfers between devices  7.5 us (7%)
  waiting for transfers between devices  1.43 us (1%)
    dot_general x16, matrix products, project(): jnp.einsum('ka,fvab,lb->fvkl', dct_basis, face_trace, dct_basis, precisio...  10.8 us
    dot_general x16, matrix products, project(): jnp.einsum('ka,fvkl,lb->fvab', dct_basis, modes * mask_grid, dct_basis, p...  10.3 us
    ppermute x4, starting transfers between devices, passed_along(): return lax.ppermute(block, axis, route)  7.5 us
    dot_general x3, matrix products, volume_rate(): jnp.einsum('wv,evijk->ewijk', flux_matrix[axis_id], along, precision=high...  6.99 us
    mul x8, local copies, waits for them, and re-layouts, project(): modes * mask_grid  5.53 us
    scatter-add x1, local copies, waits for them, and re-layouts, add_faces(): tendency = tendency.at[:, :, :, :, 0].add(scaled[4])  4.5 us
    scatter-add x1, local copies, waits for them, and re-layouts, add_faces(): tendency = tendency.at[:, :, :, :, last_index].add(scaled[5])  4.28 us
    reshape x2, local copies, waits for them, and re-layouts, on_device(): return (time_step * tendency).reshape(elem_rows, width, PTS ** 3)  3.55 us
  transfers between devices with their start and end apart: 4, of which 1 were waited for; matrix products, arithmetic and copies ran while one was open for 54% of the time, Pallas kernels for 0%

commit v1 on v0

v1 whole, which is shorter than its diff:
```python
import functools

import jax
import jax.numpy as jnp
import numpy as np
from jax import lax
from jax.experimental import pallas as pl
from jax.experimental.pallas import tpu as pltpu
from jax.sharding import PartitionSpec as P

MESH = pl.DeviceIdType.MESH
BF = jnp.bfloat16
F32 = jnp.float32
ROWS = 64
LANES = 256
TIME_STEP = 0.01


def cheb_np(n):
    idx = np.arange(n)
    x = -np.cos(np.pi * idx / (n - 1))
    c = np.where((idx == 0) | (idx == n - 1), 2.0, 1.0) * np.where(idx % 2 == 0, 1.0, -1.0)
    eye = np.eye(n)
    off = c[:, None] / c[None, :] / (x[:, None] - x[None, :] + eye) * (1.0 - eye)
    return off - np.diag(off.sum(axis=1))


def dct_np(n):
    k = np.arange(n)[:, None]
    j = np.arange(n)[None, :]
    basis = np.cos(np.pi * k * (j + 0.5) / n) * np.sqrt(2.0 / n)
    return basis * np.where(k == 0, np.sqrt(0.5), 1.0)


def hi_lo(matrix):
    full = matrix.astype(np.float32)
    hi = full.astype(BF)
    lo = (full - hi.astype(np.float32)).astype(BF)
    return np.stack([hi, lo])


def wide(matrix):
    return np.pad(matrix, ((0, 0), (0, LANES - matrix.shape[1])))


def tables(n):
    plane = n * n
    d = cheb_np(n)
    c = dct_np(n)
    eye = np.eye(n)
    along_y = np.kron(d.T, eye)
    along_z = np.kron(eye, d.T)
    deriv = hi_lo(np.concatenate([wide(along_y), wide(along_z)], axis=1))
    forward = np.kron(c.T, c.T)
    swapped = forward.reshape(plane, n, n).transpose(0, 2, 1).reshape(plane, plane)
    fwd = hi_lo(np.concatenate([wide(forward), wide(swapped)], axis=1))
    back = hi_lo(wide(np.kron(c, c)))
    lane = np.arange(LANES)
    first = np.where(lane < plane, lane // n, 999)
    second = np.where(lane < plane, lane % n, 999)
    ends = lambda v: np.where(v == 0, -1.0, np.where(v == n - 1, 1.0, 0.0))
    sign = lambda v: np.where(v % 2 == 0, 1.0, -1.0)
    lanes = np.stack(
        [first, second, ends(first), ends(second), sign(first), sign(second), first * 0, first * 0]
    ).astype(np.float32)
    return deriv, fwd, back, lanes, d


def body(
    n, diff, sizes,
    code_ref, order_ref, jac_ref, fields_ref, flux_ref, deriv_ref, fwd_ref, back_ref, lane_ref,
    out_ref,
    xf, xs, xl, zs, zl, zyz, zx, own, remote, fc, send_sem, recv_sem,
):
    width = fields_ref.shape[1]
    plane = n * n
    last = n - 1
    blk, sub = lax.axis_index("blk"), lax.axis_index("sub")
    n_blk, n_sub = sizes
    across = [
        (lax.rem(blk + n_blk - 1, n_blk), sub),
        (lax.rem(blk + 1, n_blk), sub),
        (blk, lax.rem(sub + n_sub - 1, n_sub)),
        (blk, lax.rem(sub + 1, n_sub)),
    ]
    barrier = pltpu.get_barrier_semaphore()
    for device in across:
        pl.semaphore_signal(barrier, inc=1, device_id=device, device_id_type=MESH)

    first = lane_ref[0:1, :]
    second = lane_ref[1:2, :]

    for i in range(n):
        slab = fields_ref[0, :, plane * i : plane * (i + 1)]
        slab = jnp.pad(slab, ((0, ROWS - width), (0, LANES - plane)))
        xf[i] = slab
        xs[i] = slab.astype(BF)
        xl[i] = (slab - slab.astype(BF).astype(F32)).astype(BF)
    stack = xs[...].reshape(n * ROWS, LANES)[:, :plane]
    stack_lo = xl[...].reshape(n * ROWS, LANES)[:, :plane]

    own[0] = xs[0]
    own[1] = xs[last]
    row_id = lax.broadcasted_iota(jnp.int32, (plane, LANES), 0).astype(F32)
    starts = [second, second + n * last, second * n, second * n + last]

    def trace(face):
        pick = jnp.where(row_id == starts[face - 2], 1.0, 0.0).astype(BF)
        spread = jnp.dot(stack, pick, preferred_element_type=F32).reshape(n, ROWS, LANES)
        total = jnp.zeros((ROWS, LANES), F32)
        for i in range(n):
            total = jnp.where(first == float(i), spread[i], total)
        own[face] = total.astype(BF)

    trace(2)
    trace(3)
    pl.semaphore_wait(barrier, 4)
    copies = []
    for face in range(4):
        copy = pltpu.make_async_remote_copy(
            src_ref=own.at[face],
            dst_ref=remote.at[face ^ 1],
            send_sem=send_sem.at[face],
            recv_sem=recv_sem.at[face ^ 1],
            device_id=across[face],
            device_id_type=MESH,
        )
        copy.start()
        copies.append(copy)
    trace(4)
    trace(5)

    fc[...] = jnp.zeros_like(fc)
    for axis in range(3):
        scaled = flux_ref[axis] * (-TIME_STEP * jac_ref[0, axis])
        fc[axis, 0:width, 0:width] = scaled
    flux = jnp.concatenate([fc[0], fc[1], fc[2]], axis=1)
    flux_hi = flux.astype(BF)
    flux_lo = (flux - flux_hi.astype(F32)).astype(BF)
    flux_both = jnp.concatenate([flux_hi, flux_lo], axis=0)

    zyz[...] = (
        jnp.dot(stack, deriv_ref[0], preferred_element_type=F32)
        + jnp.dot(stack, deriv_ref[1], preferred_element_type=F32)
        + jnp.dot(stack_lo, deriv_ref[0], preferred_element_type=F32)
    ).reshape(n, ROWS, 2 * LANES)

    for r in range(0, ROWS, 16):
        for c in range(0, LANES, 128):
            parts = [xf[a, r : r + 16, c : c + 128] for a in range(n)]
            for i in range(n):
                total = parts[0] * float(diff[i, 0])
                for a in range(1, n):
                    total = total + parts[a] * float(diff[i, a])
                zx[i, r : r + 16, c : c + 128] = total

    own_flat = own[...].reshape(6 * ROWS, LANES)[:, :plane]
    own_modes = (
        jnp.dot(own_flat, fwd_ref[0, :, :LANES], preferred_element_type=F32)
        + jnp.dot(own_flat, fwd_ref[1, :, :LANES], preferred_element_type=F32)
    ).reshape(6, ROWS, LANES)

    for copy in copies:
        copy.wait()

    far = jnp.concatenate([remote[...], own[5:6], own[4:5]], axis=0)
    far = far.reshape(6 * ROWS, LANES)[:, :plane]
    far_modes = (
        jnp.dot(far, fwd_ref[0], preferred_element_type=F32)
        + jnp.dot(far, fwd_ref[1], preferred_element_type=F32)
    ).reshape(6, ROWS, 2 * LANES)
    ones = jnp.ones((1, LANES), F32)
    sign_first = lane_ref[4:5, :]
    sign_second = lane_ref[5:6, :]
    modes = []
    for face in range(6):
        code = code_ref[0, face]
        order = order_ref[0, face].astype(F32)
        swap = code >= 4
        rev_a = lax.rem(lax.div(code, 2), 2)
        rev_b = lax.rem(code, 2)
        use_first = jnp.where(swap, rev_b, rev_a) == 1
        use_second = jnp.where(swap, rev_a, rev_b) == 1
        sign = jnp.where(use_first, sign_first, ones) * jnp.where(use_second, sign_second, ones)
        keep = jnp.where((first < order) & (second < order), 1.0, 0.0)
        turned = jnp.where(swap, far_modes[face, :, LANES:], far_modes[face, :, :LANES])
        modes.append((turned * sign - own_modes[face]) * keep)
    modes = jnp.concatenate(modes, axis=0)[:, :plane]
    modes_hi = modes.astype(BF)
    modes_lo = (modes - modes_hi.astype(F32)).astype(BF)
    modes = modes_hi
    jump = (
        jnp.dot(modes_lo, back_ref[0], preferred_element_type=F32)
        + jnp.dot(modes, back_ref[0], preferred_element_type=F32)
        + jnp.dot(modes, back_ref[1], preferred_element_type=F32)
    ).reshape(6, ROWS, LANES)
    lift = 0.5 * last * last * 0.5
    jump = jump * lift

    row_int = lax.broadcasted_iota(jnp.int32, (plane, LANES), 0)
    row_second = row_int - n * lax.div(row_int, n)
    col = lax.broadcasted_iota(jnp.int32, (plane, LANES), 1)
    places = [row_second, row_second + n * last, row_second * n, row_second * n + last]
    blocks = [[], [], [], []]
    for f in range(4):
        for i in range(n):
            blocks[f].append(jnp.where(first == float(i), jump[f + 2], 0.0).astype(BF))
    scat = []
    for axis in range(2):
        total = None
        for side in range(2):
            f = 2 * axis + side
            put = jnp.where(col == places[f], 1.0 if side else -1.0, 0.0).astype(BF)
            part = jnp.dot(
                jnp.concatenate(blocks[f], axis=0)[:, :plane], put, preferred_element_type=F32
            )
            total = part if total is None else total + part
        scat.append(total.reshape(n, ROWS, LANES))

    gain_y = lane_ref[2:3, :] * (TIME_STEP * jac_ref[0, 1])
    gain_z = lane_ref[3:4, :] * (TIME_STEP * jac_ref[0, 2])
    gain_x = TIME_STEP * jac_ref[0, 0]
    zx[0] = zx[0] - jump[0]
    zx[last] = zx[last] + jump[1]

    def keep_both(i, axis, value):
        hi = value.astype(BF)
        zs[i, axis] = hi
        zl[i, axis] = (value - hi.astype(F32)).astype(BF)

    for i in range(n):
        keep_both(i, 0, zx[i])
        keep_both(i, 1, zyz[i, :, :LANES] + scat[0][i])
        keep_both(i, 2, zyz[i, :, LANES:] + scat[1][i])
        both = jnp.dot(
            flux_both, zs[i].reshape(3 * ROWS, LANES), preferred_element_type=F32
        )
        moved = both[:ROWS] + both[ROWS:] + jnp.dot(
            flux_hi, zl[i].reshape(3 * ROWS, LANES), preferred_element_type=F32
        )
        moved = moved + scat[0][i] * gain_y + scat[1][i] * gain_z
        if i == 0:
            moved = moved + jump[0] * gain_x
        if i == last:
            moved = moved + jump[1] * gain_x
        out_ref[0, :, plane * i : plane * (i + 1)] = moved[:width, :plane]


def solution(mesh):
    sizes = (mesh.shape["blk"], mesh.shape["sub"])

    def on_device(fields, flux_matrix, inv_jacobian, neighbour, orientation, face_order):
        points = fields.shape[2]
        n = round(points ** (1.0 / 3.0))
        deriv, fwd, back, lanes, diff = tables(n)
        smem = pl.BlockSpec(memory_space=pltpu.SMEM)
        vmem = pl.BlockSpec(memory_space=pltpu.VMEM)
        return pl.pallas_call(
            functools.partial(body, n, diff, sizes),
            out_shape=jax.ShapeDtypeStruct(fields.shape, F32),
            in_specs=[smem] * 3 + [vmem] * 6,
            out_specs=vmem,
            scratch_shapes=[
                pltpu.VMEM((n, ROWS, LANES), F32),
                pltpu.VMEM((n, ROWS, LANES), BF),
                pltpu.VMEM((n, ROWS, LANES), BF),
                pltpu.VMEM((n, 3, ROWS, LANES), BF),
                pltpu.VMEM((n, 3, ROWS, LANES), BF),
                pltpu.VMEM((n, ROWS, 2 * LANES), F32),
                pltpu.VMEM((n, ROWS, LANES), F32),
                pltpu.VMEM((6, ROWS, LANES), BF),
                pltpu.VMEM((4, ROWS, LANES), BF),
                pltpu.VMEM((3, ROWS, ROWS), F32),
                pltpu.SemaphoreType.DMA((4,)),
                pltpu.SemaphoreType.DMA((4,)),
            ],
            compiler_params=pltpu.CompilerParams(
                collective_id=0, has_side_effects=True, vmem_limit_bytes=48 * 1024 * 1024
            ),
        )(
            orientation, face_order, inv_jacobian, fields, flux_matrix,
            jnp.asarray(deriv), jnp.asarray(fwd), jnp.asarray(back), jnp.asarray(lanes),
        )

    return jax.shard_map(
        on_device,
        mesh=mesh,
        in_specs=(
            P(("blk", "sub"), None, None),
            P(),
            P(("blk", "sub"), None),
            P(("blk", "sub"), None),
            P(("blk", "sub"), None),
            P(("blk", "sub"), None),
        ),
        out_specs=P(("blk", "sub"), None, None),
        check_vma=False,
    )
```

time: 109 us -> 14.7 us (0.13); the launches traced: 108 us -> 14.6 us
  matrix products: 37.1 us -> 0 us
  local copies, waits for them, and re-layouts: 26.6 us -> 2.64 us
  between operations: 23.7 us -> 0.06 us
  Pallas kernels: 0 us -> 11.9 us
  other arithmetic: 11.4 us -> 0 us
  starting transfers between devices: 7.5 us -> 0 us
  waiting for transfers between devices: 1.43 us -> 0 us
    dot_general x42 -> x0, matrix products: 37.1 us -> none  [the longest x16 10.8 us: project(): jnp.einsum('ka,fvab,lb->fvkl', dct_basis, face_trace, dct_basis, precisio...]
    pallas_call x0 -> x1, Pallas kernels: none -> 11.9 us  [on_device(): pl.pallas_call(functools.partial(body, n, diff, sizes), out_shape=jax.Sha...]
    scatter-add x2 -> x0, local copies, waits for them, and re-layouts: 8.77 us -> none  [the longest x1 4.5 us: add_faces(): tendency = tendency.at[:, :, :, :, 0].add(scaled[4])]
    ppermute x4 -> x0, starting transfers between devices: 7.5 us -> none  [passed_along(): return lax.ppermute(block, axis, route)]
    mul x8 -> x0, local copies, waits for them, and re-layouts: 5.53 us -> none  [project(): modes * mask_grid]
    convert_element_type x6 -> x0, other arithmetic: 4.07 us -> none  [the longest x4 2.43 us: project(): keep = (mode_index[None, :] < mode_order[:, None]).astype(jnp.float32)]
    reshape x2 -> x0, local copies, waits for them, and re-layouts: 3.55 us -> none  [on_device(): return (time_step * tendency).reshape(elem_rows, width, PTS ** 3)]
    dot_general x12 -> x0, local copies, waits for them, and re-layouts: 3.39 us -> none  [project(): jnp.einsum('ka,fvab,lb->fvkl', dct_basis, face_trace, dct_basis, precisio...]
  transfers between devices with their start and end apart: 4 -> 0, of which waited for: 1 -> 0; matrix products, arithmetic and copies ran while one was open for 54% -> 0% of each run, Pallas kernels for 0% -> 0%
where the time goes in v1:
time: 14.7 us; the launch traced here: 14.6 us
  Pallas kernels  11.9 us (81%)
  local copies, waits for them, and re-layouts  2.64 us (18%)
    pallas_call x1, Pallas kernels, on_device(): pl.pallas_call(functools.partial(body, n, diff, sizes), out_shape=jax.Sha...  11.9 us
    unnamed x17, local copies, waits for them, and re-layouts  1.33 us
    pallas_call x1, local copies, waits for them, and re-layouts, on_device(): pl.pallas_call(functools.partial(body, n, diff, sizes), out_shape=jax.Sha...  1.31 us

profile of v1, /device:TPU:0, one launch (start us, length us, event | category | flops | bytes accessed | tf_op | source)
XLA Modules:
  0.0 14.6 jit_solution(6421377789008869360)
XLA Ops:
  0.0 0.0 copy-start
  0.0 0.0 copy-start.1
  0.0 0.0 copy-start.2
  0.0 0.0 copy-start.4
  0.0 0.0 copy-start.6
  0.0 0.0 copy-start.5
  0.0 0.0 copy-start.7
  0.0 0.0 copy-start.3
  0.0 1.2 %copy.10.fields_ref = f32[1,55,2197]{2,1,0:T(8,128)S(1)} copy(f32[1,55,2197]{2,0,1:T(1,128)} %param.10) | data formatting | bytes 966680 | tf_op args[0]
  1.2 0.0 copy-done
  1.2 0.0 copy-done.1
  1.2 0.0 copy-done.2
  1.3 0.0 copy-done.4
  1.3 0.0 copy-done.6
  1.3 0.0 copy-done.5
  1.3 0.0 copy-done.7
  1.3 0.1 copy-done.3
  1.4 11.9 %shard_map.91 = f32[1,55,2197]{2,1,0:T(8,128)S(1)} custom-call(s32[1,6]{1,0:T(1,128)S(1)} %copy-done.5, s32[1,6]{1,0:T(1,128)S(1)} %copy-done.6, f32[1,3]{1,0:T(1,128)S(1)} %copy-done.7, f32[1,55,2197]{2,1,0:T(8,128)S(1)} %copy.10.fields_ref, f32[3,55,55]{2,1,0:T(8,128)S(1)} %copy-done.3, bf16[2,169,512]{2,1,0:T(8,128)(2,1)S(1)} %copy-done.1, ...), custom_call_target="tpu_custom_call" | custom-call | tf_op jit(solution)/shard_map/pallas_call | solution.py:258
  13.3 1.3 %copy.11 = f32[1,55,2197]{2,0,1:T(1,128)} copy(f32[1,55,2197]{2,1,0:T(8,128)S(1)} %shard_map.91) | data formatting | bytes 966680 | tf_op jit(solution)/shard_map/pallas_call | solution.py:258
Async XLA Ops:
  0.0 1.2 %copy-start = (bf16[2,169,512]{2,1,0:T(8,128)(2,1)S(1)}, bf16[2,169,512]{2,1,0:T(8,128)(2,1)}, u32[]{:S(2)}) copy-start(bf16[2,169,512]{2,1,0:T(8,128)(2,1)} %constant.9.clone.fwd_ref) | copy-start | bytes 1038340
  0.0 1.2 %copy-start.1 = (bf16[2,169,512]{2,1,0:T(8,128)(2,1)S(1)}, bf16[2,169,512]{2,1,0:T(8,128)(2,1)}, u32[]{:S(2)}) copy-start(bf16[2,169,512]{2,1,0:T(8,128)(2,1)} %constant.8.clone.deriv_ref) | copy-start | bytes 1038340
  0.0 1.3 %copy-start.2 = (bf16[2,169,256]{2,1,0:T(8,128)(2,1)S(1)}, bf16[2,169,256]{2,1,0:T(8,128)(2,1)}, u32[]{:S(2)}) copy-start(bf16[2,169,256]{2,1,0:T(8,128)(2,1)} %constant.10.clone.back_ref) | copy-start | bytes 519172
  0.0 1.3 %copy-start.4 = (f32[8,256]{1,0:T(8,128)S(1)}, f32[8,256]{1,0:T(8,128)}, u32[]{:S(2)}) copy-start(f32[8,256]{1,0:T(8,128)} %constant.11.clone.lane_ref) | copy-start | bytes 24580
  0.0 1.3 %copy-start.6 = (s32[1,6]{1,0:T(1,128)S(1)}, s32[1,6]{1,0:T(1,128)}, u32[]{:S(2)}) copy-start(s32[1,6]{1,0:T(1,128)} %order_ref.1) | copy-start | bytes 76
  0.0 1.3 %copy-start.5 = (s32[1,6]{1,0:T(1,128)S(1)}, s32[1,6]{1,0:T(1,128)}, u32[]{:S(2)}) copy-start(s32[1,6]{1,0:T(1,128)} %code_ref.1) | copy-start | bytes 76
  0.0 1.3 %copy-start.7 = (f32[1,3]{1,0:T(1,128)S(1)}, f32[1,3]{1,0:T(1,128)}, u32[]{:S(2)}) copy-start(f32[1,3]{1,0:T(1,128)} %jac_ref.1) | copy-start | bytes 40
  0.0 1.3 %copy-start.3 = (f32[3,55,55]{2,1,0:T(8,128)S(1)}, f32[3,55,55]{2,1,0:T(8,128)}, u32[]{:S(2)}) copy-start(f32[3,55,55]{2,1,0:T(8,128)} %flux_ref.1) | copy-start | bytes 108904

commit v2 on v1

--- a/solution.py
+++ b/solution.py
@@ -72,7 +72,7 @@
     out_ref,
     xf, xs, xl, zs, zl, zyz, zx, own, remote, fc, send_sem, recv_sem,
 ):
-    width = fields_ref.shape[1]
+    width = fields_ref.shape[0]
     plane = n * n
     last = n - 1
     blk, sub = lax.axis_index("blk"), lax.axis_index("sub")
@@ -91,7 +91,7 @@
     second = lane_ref[1:2, :]
 
     for i in range(n):
-        slab = fields_ref[0, :, plane * i : plane * (i + 1)]
+        slab = fields_ref[:, 0, plane * i : plane * (i + 1)]
         slab = jnp.pad(slab, ((0, ROWS - width), (0, LANES - plane)))
         xf[i] = slab
         xs[i] = slab.astype(BF)
@@ -148,11 +148,23 @@
     for r in range(0, ROWS, 16):
         for c in range(0, LANES, 128):
             parts = [xf[a, r : r + 16, c : c + 128] for a in range(n)]
-            for i in range(n):
-                total = parts[0] * float(diff[i, 0])
-                for a in range(1, n):
-                    total = total + parts[a] * float(diff[i, a])
-                zx[i, r : r + 16, c : c + 128] = total
+            half = n // 2
+            odd = [parts[a] - parts[last - a] for a in range(half)]
+            even = [parts[a] + parts[last - a] for a in range(half)]
+            for i in range(n - half):
+                plus = odd[0] * float(0.5 * (diff[i, 0] - diff[i, last]))
+                for a in range(1, half):
+                    plus = plus + odd[a] * float(0.5 * (diff[i, a] - diff[i, last - a]))
+                if i == last - i:
+                    zx[i, r : r + 16, c : c + 128] = plus
+                    continue
+                minus = even[0] * float(0.5 * (diff[i, 0] + diff[i, last]))
+                for a in range(1, half):
+                    minus = minus + even[a] * float(0.5 * (diff[i, a] + diff[i, last - a]))
+                if n % 2:
+                    minus = minus + parts[half] * float(diff[i, half])
+                zx[i, r : r + 16, c : c + 128] = plus + minus
+                zx[last - i, r : r + 16, c : c + 128] = plus - minus
 
     own_flat = own[...].reshape(6 * ROWS, LANES)[:, :plane]
     own_modes = (
@@ -243,7 +255,7 @@
             moved = moved + jump[0] * gain_x
         if i == last:
             moved = moved + jump[1] * gain_x
-        out_ref[0, :, plane * i : plane * (i + 1)] = moved[:width, :plane]
+        out_ref[:, 0, plane * i : plane * (i + 1)] = moved[:width, :plane]
 
 
 def solution(mesh):
@@ -255,9 +267,10 @@
         deriv, fwd, back, lanes, diff = tables(n)
         smem = pl.BlockSpec(memory_space=pltpu.SMEM)
         vmem = pl.BlockSpec(memory_space=pltpu.VMEM)
-        return pl.pallas_call(
+        turned = jnp.swapaxes(fields, 0, 1)
+        result = pl.pallas_call(
             functools.partial(body, n, diff, sizes),
-            out_shape=jax.ShapeDtypeStruct(fields.shape, F32),
+            out_shape=jax.ShapeDtypeStruct(turned.shape, F32),
             in_specs=[smem] * 3 + [vmem] * 6,
             out_specs=vmem,
             scratch_shapes=[
@@ -278,9 +291,10 @@
                 collective_id=0, has_side_effects=True, vmem_limit_bytes=48 * 1024 * 1024
             ),
         )(
-            orientation, face_order, inv_jacobian, fields, flux_matrix,
+            orientation, face_order, inv_jacobian, turned, flux_matrix,
             jnp.asarray(deriv), jnp.asarray(fwd), jnp.asarray(back), jnp.asarray(lanes),
         )
+        return jnp.swapaxes(result, 0, 1)
 
     return jax.shard_map(
         on_device,

time: 14.7 us -> 19.7 us (1.34); the launches traced: 14.6 us -> 19.3 us
  local copies, waits for them, and re-layouts: 2.64 us -> 6.98 us
  Pallas kernels: 11.9 us -> 12.3 us
    unnamed x17 -> x19, local copies, waits for them, and re-layouts: 1.33 us -> 6.98 us
    pallas_call x1 -> x0, local copies, waits for them, and re-layouts: 1.31 us -> none  [on_device(): pl.pallas_call(functools.partial(body, n, diff, sizes), out_shape=jax.Sha...]
    pallas_call x1, Pallas kernels: 11.9 us -> 12.3 us  [on_device(): pl.pallas_call(functools.partial(body, n, diff, sizes), out_shape=jax.Sha...]
where the time goes in v2:
time: 19.7 us; the launch traced here: 19.3 us
  Pallas kernels  12.3 us (62%)
  local copies, waits for them, and re-layouts  6.98 us (35%)
    pallas_call x1, Pallas kernels, on_device(): pl.pallas_call(functools.partial(body, n, diff, sizes), out_shape=jax.Sha...  12.3 us
    unnamed x19, local copies, waits for them, and re-layouts  6.98 us

profile of v2, /device:TPU:0, one launch (start us, length us, event | category | flops | bytes accessed | tf_op | source)
XLA Modules:
  0.0 19.3 jit_solution(10498936622579667876)
XLA Ops:
  0.0 0.0 copy-start.7
  0.0 0.0 copy-start.6
  0.0 0.0 copy-start.8
  0.0 0.6 %copy-done.7 = s32[1,6]{1,0:T(1,128)S(1)} copy-done((s32[1,6]{1,0:T(1,128)S(1)}, s32[1,6]{1,0:T(1,128)}, u32[]{:S(2)}) %copy-start.7) | copy-done | bytes 48
  0.7 0.0 copy-done.6
  0.7 0.0 copy-done.8
  0.7 0.0 copy-start
  0.7 1.0 %copy-done = f32[1,55,2197]{2,0,1:T(1,128)S(1)} copy-done((f32[1,55,2197]{2,0,1:T(1,128)S(1)}, f32[1,55,2197]{2,0,1:T(1,128)}, u32[]{:S(2)}) %copy-start) | copy-done | bytes 483364
  1.7 0.0 copy-start.1
  1.7 1.0 %copy-done.1 = bf16[2,169,512]{2,1,0:T(8,128)(2,1)S(1)} copy-done((bf16[2,169,512]{2,1,0:T(8,128)(2,1)S(1)}, bf16[2,169,512]{2,1,0:T(8,128)(2,1)}, u32[]{:S(2)}) %copy-start.1) | copy-done | bytes 346136
  2.7 0.0 copy-start.2
  2.7 1.0 %copy-done.2 = bf16[2,169,512]{2,1,0:T(8,128)(2,1)S(1)} copy-done((bf16[2,169,512]{2,1,0:T(8,128)(2,1)S(1)}, bf16[2,169,512]{2,1,0:T(8,128)(2,1)}, u32[]{:S(2)}) %copy-start.2) | copy-done | bytes 346136
  3.7 0.0 copy-start.3
  3.7 0.9 %copy-done.3 = bf16[2,169,256]{2,1,0:T(8,128)(2,1)S(1)} copy-done((bf16[2,169,256]{2,1,0:T(8,128)(2,1)S(1)}, bf16[2,169,256]{2,1,0:T(8,128)(2,1)}, u32[]{:S(2)}) %copy-start.3) | copy-done | bytes 173080
  4.6 0.0 copy-start.4
  4.6 0.9 %copy-done.4 = f32[3,55,55]{2,1,0:T(8,128)S(1)} copy-done((f32[3,55,55]{2,1,0:T(8,128)S(1)}, f32[3,55,55]{2,1,0:T(8,128)}, u32[]{:S(2)}) %copy-start.4) | copy-done | bytes 36324
  5.5 0.0 copy-start.5
  5.5 0.7 %copy-done.5 = f32[8,256]{1,0:T(8,128)S(1)} copy-done((f32[8,256]{1,0:T(8,128)S(1)}, f32[8,256]{1,0:T(8,128)}, u32[]{:S(2)}) %copy-start.5) | copy-done | bytes 8216
  6.2 12.3 %shard_map.91 = f32[55,1,2197]{2,1,0:T(1,128)S(1)} custom-call(s32[1,6]{1,0:T(1,128)S(1)} %copy-done.6, s32[1,6]{1,0:T(1,128)S(1)} %copy-done.7, f32[1,3]{1,0:T(1,128)S(1)} %copy-done.8, f32[55,1,2197]{2,1,0:T(1,128)S(1)} %bitcast.3, f32[3,55,55]{2,1,0:T(8,128)S(1)} %copy-done.4, bf16[2,169,512]{2,1,0:T(8,128)(2,1)S(1)} %copy-done.2, ...), custom_call_target="tpu_custom_call" | custom-call | tf_op jit(solution)/shard_map/pallas_call | solution.py:271
  18.5 0.8 %copy.11 = f32[1,55,2197]{2,0,1:T(1,128)} copy(f32[1,55,2197]{2,0,1:T(1,128)S(1)} %bitcast.2) | data formatting | bytes 966680
Async XLA Ops:
  0.0 0.7 %copy-start.7 = (s32[1,6]{1,0:T(1,128)S(1)}, s32[1,6]{1,0:T(1,128)}, u32[]{:S(2)}) copy-start(s32[1,6]{1,0:T(1,128)} %order_ref.1) | copy-start | bytes 76
  0.0 0.7 %copy-start.6 = (s32[1,6]{1,0:T(1,128)S(1)}, s32[1,6]{1,0:T(1,128)}, u32[]{:S(2)}) copy-start(s32[1,6]{1,0:T(1,128)} %code_ref.1) | copy-start | bytes 76
  0.0 0.7 %copy-start.8 = (f32[1,3]{1,0:T(1,128)S(1)}, f32[1,3]{1,0:T(1,128)}, u32[]{:S(2)}) copy-start(f32[1,3]{1,0:T(1,128)} %jac_ref.1) | copy-start | bytes 40
  0.7 1.0 %copy-start = (f32[1,55,2197]{2,0,1:T(1,128)S(1)}, f32[1,55,2197]{2,0,1:T(1,128)}, u32[]{:S(2)}) copy-start(f32[1,55,2197]{2,0,1:T(1,128)} %param.10) | copy-start | bytes 1450024
  1.7 1.0 %copy-start.1 = (bf16[2,169,512]{2,1,0:T(8,128)(2,1)S(1)}, bf16[2,169,512]{2,1,0:T(8,128)(2,1)}, u32[]{:S(2)}) copy-start(bf16[2,169,512]{2,1,0:T(8,128)(2,1)} %constant.9.clone.fwd_ref) | copy-start | bytes 1038340
  2.7 1.0 %copy-start.2 = (bf16[2,169,512]{2,1,0:T(8,128)(2,1)S(1)}, bf16[2,169,512]{2,1,0:T(8,128)(2,1)}, u32[]{:S(2)}) copy-start(bf16[2,169,512]{2,1,0:T(8,128)(2,1)} %constant.8.clone.deriv_ref) | copy-start | bytes 1038340
  3.7 0.9 %copy-start.3 = (bf16[2,169,256]{2,1,0:T(8,128)(2,1)S(1)}, bf16[2,169,256]{2,1,0:T(8,128)(2,1)}, u32[]{:S(2)}) copy-start(bf16[2,169,256]{2,1,0:T(8,128)(2,1)} %constant.10.clone.back_ref) | copy-start | bytes 519172
  4.6 0.9 %copy-start.4 = (f32[3,55,55]{2,1,0:T(8,128)S(1)}, f32[3,55,55]{2,1,0:T(8,128)}, u32[]{:S(2)}) copy-start(f32[3,55,55]{2,1,0:T(8,128)} %flux_ref.1) | copy-start | bytes 108904
  5.5 0.7 %copy-start.5 = (f32[8,256]{1,0:T(8,128)S(1)}, f32[8,256]{1,0:T(8,128)}, u32[]{:S(2)}) copy-start(f32[8,256]{1,0:T(8,128)} %constant.11.clone.lane_ref) | copy-start | bytes 24580
